TPU v7x, 32 devices: a whole 2x2x4 slice. The times are simulated.
32 devices in a mesh: grp: 2 (over y), blk: 4 (over z), sub: 2 (over x), pair: 2 (over core).
Axes of the slice: x: 2, y: 2, z: 4, core: 2. Of those that a mesh axis runs over, the one named last changes fastest.
Arguments:
- grad_volume: bfloat16 [16, 128, 8192], P(('grp', 'blk', 'sub'), 'pair'), parts along dimension 0, may hold values from -6 to 6
- query_feats: bfloat16 [16384, 1024], P(('grp', 'blk')), parts along dimension 0, may hold values from -6 to 6
- support_feats: bfloat16 [16, 128, 1024], P(('grp', 'blk', 'sub'), 'pair'), parts along dimension 0, may hold values from -6 to 6
- query_kernel: float32 [3, 3], replicated, may hold values from -2 to 2
- support_kernel: float32 [3, 3], replicated, may hold values from -2 to 2
Outputs:
- query_grad: float32 [16384, 1024], P(('grp', 'blk', 'sub', 'pair')), parts along dimension 0
- support_grad: float32 [16, 128, 1024], P(('grp', 'blk', 'sub'), 'pair'), parts along dimension 0
There are 2 independent parts, one for each index of `grp`. A program takes and returns all parts, laid end to end along the dimension named above; an argument that names none is the same for every part. Nothing has to cross between parts.
All inputs are finite; a program needn't handle non-finite values.
Results may differ from a plain program's by a relative error of at most 0.0029.
Values may be sent and summed in bfloat16 or wider, within the bound.
No kernel may reach another device: no remote copies, remote signals or barrier semaphores. Data moves between devices by JAX's collectives and lax.ppermute only.
A program may use at most 64 MiB of HBM per device.

v0:
```python
import math
import jax
import jax.numpy as jnp
from jax import lax
from jax.sharding import PartitionSpec as P

QW = 128
QH = 64


def extended(cells, sides, width):
    for axis, dim in sides:
        count = lax.axis_size(axis)
        ends = count - 1
        head = lax.slice_in_dim(cells, 0, width, axis=dim)
        tail = lax.slice_in_dim(cells, cells.shape[dim] - width, cells.shape[dim], axis=dim)
        cells = jnp.concatenate(
            [
                lax.ppermute(tail, axis, [(i, (i + 1) % count) for i in range(ends)]),
                cells,
                lax.ppermute(head, axis, [((i + 1) % count, i) for i in range(ends)]),
            ],
            axis=dim,
        )
    return cells


def shifted(value, axis, steps):
    count = lax.axis_size(axis)
    pairs = [(source, (source + steps) % count) for source in range(count)]
    return lax.ppermute(value, axis, pairs)


def query_pass(volume, kernel):
    planes, columns, queries = volume.shape
    grid = volume.astype(jnp.float32).reshape(planes, columns, QH, QW)
    padded = jnp.pad(grid, ((0, 0), (0, 0), (1, 1), (1, 1)))
    total = jnp.zeros_like(grid)
    for row_shift in range(3):
        for col_shift in range(3):
            total = (
                total
                + kernel[row_shift, col_shift]
                * padded[:, :, row_shift : row_shift + QH, col_shift : col_shift + QW]
            )
    return total.reshape(planes, columns, queries)


def support_pass(rimmed, kernel, planes, columns):
    total = jnp.zeros((planes, columns, rimmed.shape[2]), jnp.float32)
    for row_shift in range(3):
        for col_shift in range(3):
            total = total + kernel[row_shift, col_shift] * rimmed[
                row_shift : row_shift + planes, col_shift : col_shift + columns
            ].astype(jnp.float32)
    return total


def shards(grad_volume, query_feats, support_feats, query_kernel, support_kernel):
    planes, columns, queries = grad_volume.shape
    rimmed = extended(grad_volume, ((("blk", "sub"), 0), ("pair", 1)), 1)
    corr_grad = (
        query_pass(grad_volume, query_kernel)
        + support_pass(rimmed, support_kernel, planes, columns)
    ).astype(jnp.bfloat16)
    moved = lax.all_to_all(corr_grad, "blk", split_axis=2, concat_axis=0, tiled=True)
    cycle_size = lax.axis_size("blk")
    own_index = lax.axis_index("blk")
    tile_len = moved.shape[2]
    tiles = moved.reshape(cycle_size, planes, columns, tile_len)
    width = query_feats.shape[1]
    scale_factor = 1.0 / math.sqrt(width)

    def project(piece_index, feat_piece, acc_piece, count):
        whole_block = lax.dynamic_index_in_dim(tiles, piece_index, 0, keepdims=False)
        block = whole_block.reshape(planes * count, tile_len)
        feat_flat = feat_piece.reshape(planes * count, width)
        query_term = lax.dot_general(
            block, feat_flat, (((0,), (0,)), ((), ())), preferred_element_type=jnp.float32
        )
        acc_new = acc_piece + jnp.dot(
            block, query_feats, preferred_element_type=jnp.float32
        ).reshape(planes, count, width)
        return (query_term, acc_new)

    query_start = jnp.zeros((tile_len, width), jnp.float32)

    def turn_one(turn_index, carry):
        query_total, feat_piece, acc_piece = carry
        term_piece, acc_piece = project(
            (own_index - turn_index) % cycle_size, feat_piece, acc_piece, columns
        )
        feat_piece = shifted(feat_piece, "blk", 1)
        acc_piece = shifted(acc_piece, "blk", 1)
        return (query_total + term_piece, feat_piece, acc_piece)

    start = (query_start, support_feats, jnp.zeros((planes, columns, width), jnp.float32))
    query_total, feat_piece, support_total = lax.fori_loop(0, cycle_size, turn_one, start)
    query_grad = (
        lax.psum_scatter(query_total, ("sub", "pair"), scatter_dimension=0, tiled=True)
        * scale_factor
    )
    return (query_grad, support_total * scale_factor)


def solution(mesh):
    in_specs = (
        P(("grp", "blk", "sub"), "pair", None),
        P(("grp", "blk"), None),
        P(("grp", "blk", "sub"), "pair", None),
        P(),
        P(),
    )
    out_specs = (P(("grp", "blk", "sub", "pair"), None), P(("grp", "blk", "sub"), "pair", None))
    return jax.shard_map(shards, mesh=mesh, in_specs=in_specs, out_specs=out_specs, check_vma=False)
```

profile of v0, /device:TPU:0, one launch (start us, length us, event | category | flops | bytes accessed | tf_op | source)
XLA Modules:
  0.0 318.6 jit_solution(11927447084421412007)
XLA Ops:
  7.2 5.0 %collective-permute-start.2 = (bf16[1,64,8192]{2,1,0:T(8,128)(2,1)}, bf16[1,64,8192]{2,1,0:T(8,128)(2,1)S(1)}, u32[]{:S(2)}, u32[]{:S(2)}) collective-permute-start(bf16[1,64,8192]{2,1,0:T(8,128)(2,1)} %param.7), channel_id=1, source_target_pairs={{0,2},{2,4},{4,6},{6,8},{8,10},{10,12},{12,14},{1,3},{3,5},{5,7},{... | collective-permute-start | bytes 3145736 | tf_op jit(solution)/shard_map/ppermute | solution.py:19
  12.2 1.3 collective-permute-start.3
  13.5 1.7 fusion.33
  15.2 1.7 fusion.32
  16.9 40.4 %collective-permute-done.2 = bf16[1,64,8192]{2,1,0:T(8,128)(2,1)S(1)} collective-permute-done((bf16[1,64,8192]{2,1,0:T(8,128)(2,1)}, bf16[1,64,8192]{2,1,0:T(8,128)(2,1)S(1)}, u32[]{:S(2)}, u32[]{:S(2)}) %collective-permute-start.2) | collective-permute-done | bytes 1048608 | tf_op jit(solution)/shard_map/ppermute | solution.py:19
  58.1 1.3 collective-permute-start.5
  59.4 3.0 collective-permute-start.4
  62.8 9.4 %fusion.23 = f32[1,64,64,128]{3,2,1,0:T(8,128)S(1)} fusion(f32[1,64,64,128]{3,2,1,0:T(8,128)S(1)} %bitcast.53, f32[]{:T(128)} %bitcast.8, f32[]{:T(128)} %bitcast.7, f32[]{:T(128)} %bitcast.6, f32[]{:T(128)} %bitcast.5, f32[]{:T(128)} %bitcast.4, f32[]{:T(128)} %bitcast.3, f32[]{:T(128)} %bitcast.2, f32[]{:T(128)} %bitcast.1, f32[]{:T(128)} %bitcast), kind=kLoop, calls=%fused_computation.35 | loop fusion | flops 8912896 | bytes 4194340 | tf_op jit(solution)/shard_map/add | solution.py:42
  72.3 1.5 reshape.56
  74.0 11.4 %fusion.14 = bf16[1,64,8192]{2,1,0:T(8,128)(2,1)S(1)} fusion(f32[1,64,8192]{2,1,0:T(8,128)} %reshape.56, bf16[1,64,8192]{2,1,0:T(8,128)(2,1)} %param.7, bf16[1,64,8192]{2,1,0:T(8,128)(2,1)} %copy-done.2, bf16[1,64,8192]{2,1,0:T(8,128)(2,1)S(1)} %collective-permute-done.2, bf16[3,1,8192]{2,1,0:T(2,128)(2,1)S(1)} %copy.17, bf16[3,64,8192]{2,1,0:T(8,128)(2,1)} %copy-done, ...), kind=kLoop, calls=%fused_computation.26 | loop fusion | flops 24117248 | bytes 9535524 | tf_op jit(solution)/shard_map/convert_element_type | solution.py:65
  85.4 6.8 %copy.18 = bf16[1,64,8192]{1,0,2:T(2,128)(2,1)} copy(bf16[1,64,8192]{2,1,0:T(8,128)(2,1)S(1)} %fusion.14) | data formatting | bytes 2097152 | tf_op jit(solution)/shard_map/convert_element_type | solution.py:65
  92.7 45.2 %reduce = bf16[8192,64]{1,0:T(8,128)(2,1)S(1)} reduce(bf16[8192,1,64]{2,1,0:T(2,128)(2,1)} %bitcast.51, bf16[]{:T(256)} %broadcast.17), dimensions={1}, to_apply=%bitcast.38.reduce_sub_computation | reduce | bytes 2097154
  138.0 2.7 reshape.60
  140.6 6.3 %all-to-all-start = ((bf16[4,2,65536]{2,1,0:T(2,128)(2,1)}), bf16[4,2,65536]{2,1,0:T(2,128)(2,1)S(1)}, u32[]{:S(2)}, u32[]{:S(2)}) async-start(bf16[4,2,65536]{2,1,0:T(2,128)(2,1)} %reshape.60), calls=%async_computation | async-start | bytes 2097152 | tf_op jit(solution)/shard_map/all_to_all | solution.py:66
  146.9 25.3 %all-to-all-done = bf16[4,2,65536]{2,1,0:T(2,128)(2,1)S(1)} async-done(((bf16[4,2,65536]{2,1,0:T(2,128)(2,1)}), bf16[4,2,65536]{2,1,0:T(2,128)(2,1)S(1)}, u32[]{:S(2)}, u32[]{:S(2)}) %all-to-all-start) | async-done | bytes 1048608 | tf_op jit(solution)/shard_map/all_to_all | solution.py:66
  172.2 3.2 reshape.61
  175.4 8.2 %copy.19 = bf16[1,64,8192]{2,1,0:T(8,128)(2,1)S(1)} copy(bf16[1,64,8192]{1,0,2:T(2,128)(2,1)} %bitcast.52) | data formatting | bytes 2097152 | tf_op jit(solution)/shard_map/all_to_all | solution.py:66
  185.0 52.0 %while.20 = (s32[]{:T(128)}, f32[2048,1024]{1,0:T(8,128)}, bf16[1,64,1024]{2,1,0:T(8,128)(2,1)S(1)}, f32[1,64,1024]{2,1,0:T(8,128)S(1)}, s32[]{:T(128)}, /*index...) while((s32[]{:T(128)}, f32[2048,1024]{1,0:T(8,128)}, ...), condition=%wide.region_1.2_spmd.clone, body=%wide.region_0.1_spmd.clone.sunk | while | flops 541130752 | bytes 23986536 | solution.py:98
  185.1 3.0 fusion.44
  188.4 4.5 %select_add_fusion.2 = f32[2048,1024]{1,0:T(8,128)} fusion(f32[2048,1024]{1,0:T(8,128)} %get-tuple-element.318, pred[]{:T(512)S(6)} %compare.5, bf16[4,1,64,2048]{3,2,1,0:T(8,128)(2,1)S(1)} %get-tuple-element.333, s32[]{:T(128)S(6)} %select_n.36, bf16[1,64,1024]{2,1,0:T(8,128)(2,1)S(1)} %copy.32), kind=kOutput, calls=%fused_computation.clone.1 | convolution fusion | flops 272629760 | bytes 17170436 | tf_op jit(solution)/shard_map/while/body/eval_jaxpr/dot_general | solution.py:78
  192.9 4.6 %collective-permute-done.1 = f32[1,64,1024]{2,1,0:T(8,128)S(1)} collective-permute-done((f32[1,64,1024]{2,1,0:T(8,128)S(1)}, f32[1,64,1024]{2,1,0:T(8,128)S(1)}, u32[]{:S(2)}, u32[]{:S(2)}) %collective-permute-start.1) | collective-permute-done | bytes 262176 | tf_op jit(solution)/shard_map/while/body/eval_jaxpr/ppermute | solution.py:31
  197.5 3.0 fusion.44
  200.8 7.9 %select_add_fusion.2 = f32[2048,1024]{1,0:T(8,128)} fusion(f32[2048,1024]{1,0:T(8,128)} %get-tuple-element.318, pred[]{:T(512)S(6)} %compare.5, bf16[4,1,64,2048]{3,2,1,0:T(8,128)(2,1)S(1)} %get-tuple-element.333, s32[]{:T(128)S(6)} %select_n.36, bf16[1,64,1024]{2,1,0:T(8,128)(2,1)S(1)} %copy.32), kind=kOutput, calls=%fused_computation.clone.1 | convolution fusion | flops 272629760 | bytes 17170436 | tf_op jit(solution)/shard_map/while/body/eval_jaxpr/dot_general | solution.py:78
  209.9 1.3 collective-permute-start
  211.2 3.0 fusion.44
  214.2 2.4 collective-permute-start.1
  216.6 7.9 %select_add_fusion.2 = f32[2048,1024]{1,0:T(8,128)} fusion(f32[2048,1024]{1,0:T(8,128)} %get-tuple-element.318, pred[]{:T(512)S(6)} %compare.5, bf16[4,1,64,2048]{3,2,1,0:T(8,128)(2,1)S(1)} %get-tuple-element.333, s32[]{:T(128)S(6)} %select_n.36, bf16[1,64,1024]{2,1,0:T(8,128)(2,1)S(1)} %copy.32), kind=kOutput, calls=%fused_computation.clone.1 | convolution fusion | flops 272629760 | bytes 17170436 | tf_op jit(solution)/shard_map/while/body/eval_jaxpr/dot_general | solution.py:78
  224.6 3.0 fusion.44
  227.6 1.4 collective-permute-start.1
  229.0 7.9 %select_add_fusion.2 = f32[2048,1024]{1,0:T(8,128)} fusion(f32[2048,1024]{1,0:T(8,128)} %get-tuple-element.318, pred[]{:T(512)S(6)} %compare.5, bf16[4,1,64,2048]{3,2,1,0:T(8,128)(2,1)S(1)} %get-tuple-element.333, s32[]{:T(128)S(6)} %select_n.36, bf16[1,64,1024]{2,1,0:T(8,128)(2,1)S(1)} %copy.32), kind=kOutput, calls=%fused_computation.clone.1 | convolution fusion | flops 272629760 | bytes 17170436 | tf_op jit(solution)/shard_map/while/body/eval_jaxpr/dot_general | solution.py:78
  237.7 70.9 %reduce-scatter.2.cloned.1.call-done = f32[512,1024]{1,0:T(8,128)} async-done(((f32[2048,1024]{1,0:T(8,128)}), f32[512,1024]{1,0:T(8,128)}) %reduce-scatter.2.cloned.1.call-update) | async-done | bytes 2097168 | tf_op jit(solution)/shard_map/reduce_scatter | solution.py:100
  308.5 3.2 %broadcast_multiply_fusion = f32[512,1024]{1,0:T(8,128)} fusion(f32[512,1024]{1,0:T(8,128)} %reduce-scatter.2.cloned.1.call-done), kind=kLoop, calls=%fused_computation.45 | loop fusion | flops 524288 | bytes 4194304 | tf_op jit(solution)/shard_map/mul | solution.py:100
  (44 shorter events, 5.8 us)
Async XLA Ops:
  7.2 50.3 %copy-start.3 = (bf16[1,64,8192]{2,1,0:T(8,128)(2,1)S(1)}, bf16[1,64,8192]{2,1,0:T(8,128)(2,1)}, u32[]{:S(2)}) copy-start(bf16[1,64,8192]{2,1,0:T(8,128)(2,1)} %param.7) | copy-start | bytes 3145732
  7.2 50.2 %collective-permute-start.2 = (bf16[1,64,8192]{2,1,0:T(8,128)(2,1)}, bf16[1,64,8192]{2,1,0:T(8,128)(2,1)S(1)}, u32[]{:S(2)}, u32[]{:S(2)}) collective-permute-start(bf16[1,64,8192]{2,1,0:T(8,128)(2,1)} %param.7), channel_id=1, source_target_pairs={{0,2},{2,4},{4,6},{6,8},{8,10},{10,12},{12,14},{1,3},{3,5},{5,7},{... | collective-permute-start | bytes 3145736 | tf_op jit(solution)/shard_map/ppermute | solution.py:19
  12.2 45.5 %collective-permute-start.3 = (bf16[1,64,8192]{2,1,0:T(8,128)(2,1)}, bf16[1,64,8192]{2,1,0:T(8,128)(2,1)S(1)}, u32[]{:S(2)}, u32[]{:S(2)}) collective-permute-start(bf16[1,64,8192]{2,1,0:T(8,128)(2,1)} %param.7), channel_id=1, source_target_pairs={{2,0},{4,2},{6,4},{8,6},{10,8},{12,10},{14,12},{3,1},{5,3},{7,5},{... | collective-permute-start | bytes 3145736 | tf_op jit(solution)/shard_map/ppermute | solution.py:21
  57.7 5.1 %copy-start.2 = (bf16[1,64,8192]{2,1,0:T(8,128)(2,1)}, bf16[1,64,8192]{2,1,0:T(8,128)(2,1)S(1)}, u32[]{:S(2)}) copy-start(bf16[1,64,8192]{2,1,0:T(8,128)(2,1)S(1)} %collective-permute-done.3) | copy-start | bytes 3145732
  57.8 5.1 %copy-start = (bf16[3,64,8192]{2,1,0:T(8,128)(2,1)}, bf16[3,64,8192]{2,1,0:T(8,128)(2,1)S(1)}, u32[]{:S(2)}) copy-start(bf16[3,64,8192]{2,1,0:T(8,128)(2,1)S(1)} %constant_dynamic-update-slice_fusion) | copy-start | bytes 9437188
  58.1 15.7 %collective-permute-start.5 = (bf16[3,1,8192]{2,0,1:T(4,128)(2,1)S(1)}, bf16[3,1,8192]{2,0,1:T(4,128)(2,1)S(1)}, u32[]{:S(2)}, u32[]{:S(2)}) collective-permute-start(bf16[3,1,8192]{2,0,1:T(4,128)(2,1)S(1)} %copy.22), channel_id=1, source_target_pairs={{1,0},{3,2},{5,4},{7,6},{9,8},{11,10},{13,12},{15,14},{17,16},{19,... | collective-permute-start | bytes 147464 | tf_op jit(solution)/shard_map/ppermute | solution.py:21
  59.4 14.5 %collective-permute-start.4 = (bf16[3,1,8192]{2,0,1:T(4,128)(2,1)S(1)}, bf16[3,1,8192]{2,0,1:T(4,128)(2,1)S(1)}, u32[]{:S(2)}, u32[]{:S(2)}) collective-permute-start(bf16[3,1,8192]{2,0,1:T(4,128)(2,1)S(1)} %copy.21), channel_id=1, source_target_pairs={{0,1},{2,3},{4,5},{6,7},{8,9},{10,11},{12,13},{14,15},{16,17},{18,... | collective-permute-start | bytes 147464 | tf_op jit(solution)/shard_map/ppermute | solution.py:19
  140.6 31.6 %all-to-all-start = ((bf16[4,2,65536]{2,1,0:T(2,128)(2,1)}), bf16[4,2,65536]{2,1,0:T(2,128)(2,1)S(1)}, u32[]{:S(2)}, u32[]{:S(2)}) async-start(bf16[4,2,65536]{2,1,0:T(2,128)(2,1)} %reshape.60), calls=%async_computation | async-start | bytes 2097152 | tf_op jit(solution)/shard_map/all_to_all | solution.py:66
  146.9 161.6 %reduce-scatter.2.cloned.1.call-start = ((), (), s32[]{:S(2)}) async-start(), calls=%async_computation.2 | async-start | bytes 10485760 | tf_op jit(solution)/shard_map/reduce_scatter | solution.py:100
  183.5 1.4 copy-start.1
  185.0 7.9 %collective-permute-start = (bf16[1,64,1024]{2,1,0:T(8,128)(2,1)S(1)}, bf16[1,64,1024]{2,1,0:T(8,128)(2,1)S(1)}, u32[]{:S(2)}, u32[]{:S(2)}) collective-permute-start(bf16[1,64,1024]{2,1,0:T(8,128)(2,1)S(1)} %copy.32), channel_id=1, source_target_pairs={{0,4},{4,8},{8,12},{12,0},{1,5},{5,9},{9,13},{13,1},{2,6},{6,10},{... | collective-permute-start | bytes 393224 | tf_op jit(solution)/shard_map/while/body/eval_jaxpr/ppermute | solution.py:31
  188.1 9.3 %collective-permute-start.1 = (f32[1,64,1024]{2,1,0:T(8,128)S(1)}, f32[1,64,1024]{2,1,0:T(8,128)S(1)}, u32[]{:S(2)}, u32[]{:S(2)}) collective-permute-start(f32[1,64,1024]{2,1,0:T(8,128)S(1)} %fusion.44), channel_id=1, source_target_pairs={{0,4},{4,8},{8,12},{12,0},{1,5},{5,9},{9,13},{13,1},{2,6},{6,10},{... | collective-permute-start | bytes 786440 | tf_op jit(solution)/shard_map/while/body/eval_jaxpr/ppermute | solution.py:31
  197.4 11.2 %collective-permute-start = (bf16[1,64,1024]{2,1,0:T(8,128)(2,1)S(1)}, bf16[1,64,1024]{2,1,0:T(8,128)(2,1)S(1)}, u32[]{:S(2)}, u32[]{:S(2)}) collective-permute-start(bf16[1,64,1024]{2,1,0:T(8,128)(2,1)S(1)} %copy.32), channel_id=1, source_target_pairs={{0,4},{4,8},{8,12},{12,0},{1,5},{5,9},{9,13},{13,1},{2,6},{6,10},{... | collective-permute-start | bytes 393224 | tf_op jit(solution)/shard_map/while/body/eval_jaxpr/ppermute | solution.py:31
  200.6 9.3 %collective-permute-start.1 = (f32[1,64,1024]{2,1,0:T(8,128)S(1)}, f32[1,64,1024]{2,1,0:T(8,128)S(1)}, u32[]{:S(2)}, u32[]{:S(2)}) collective-permute-start(f32[1,64,1024]{2,1,0:T(8,128)S(1)} %fusion.44), channel_id=1, source_target_pairs={{0,4},{4,8},{8,12},{12,0},{1,5},{5,9},{9,13},{13,1},{2,6},{6,10},{... | collective-permute-start | bytes 786440 | tf_op jit(solution)/shard_map/while/body/eval_jaxpr/ppermute | solution.py:31
  209.9 14.6 %collective-permute-start = (bf16[1,64,1024]{2,1,0:T(8,128)(2,1)S(1)}, bf16[1,64,1024]{2,1,0:T(8,128)(2,1)S(1)}, u32[]{:S(2)}, u32[]{:S(2)}) collective-permute-start(bf16[1,64,1024]{2,1,0:T(8,128)(2,1)S(1)} %copy.32), channel_id=1, source_target_pairs={{0,4},{4,8},{8,12},{12,0},{1,5},{5,9},{9,13},{13,1},{2,6},{6,10},{... | collective-permute-start | bytes 393224 | tf_op jit(solution)/shard_map/while/body/eval_jaxpr/ppermute | solution.py:31
  214.2 10.3 %collective-permute-start.1 = (f32[1,64,1024]{2,1,0:T(8,128)S(1)}, f32[1,64,1024]{2,1,0:T(8,128)S(1)}, u32[]{:S(2)}, u32[]{:S(2)}) collective-permute-start(f32[1,64,1024]{2,1,0:T(8,128)S(1)} %fusion.44), channel_id=1, source_target_pairs={{0,4},{4,8},{8,12},{12,0},{1,5},{5,9},{9,13},{13,1},{2,6},{6,10},{... | collective-permute-start | bytes 786440 | tf_op jit(solution)/shard_map/while/body/eval_jaxpr/ppermute | solution.py:31
  224.5 12.4 %collective-permute-start = (bf16[1,64,1024]{2,1,0:T(8,128)(2,1)S(1)}, bf16[1,64,1024]{2,1,0:T(8,128)(2,1)S(1)}, u32[]{:S(2)}, u32[]{:S(2)}) collective-permute-start(bf16[1,64,1024]{2,1,0:T(8,128)(2,1)S(1)} %copy.32), channel_id=1, source_target_pairs={{0,4},{4,8},{8,12},{12,0},{1,5},{5,9},{9,13},{13,1},{2,6},{6,10},{... | collective-permute-start | bytes 393224 | tf_op jit(solution)/shard_map/while/body/eval_jaxpr/ppermute | solution.py:31
  227.6 9.3 %collective-permute-start.1 = (f32[1,64,1024]{2,1,0:T(8,128)S(1)}, f32[1,64,1024]{2,1,0:T(8,128)S(1)}, u32[]{:S(2)}, u32[]{:S(2)}) collective-permute-start(f32[1,64,1024]{2,1,0:T(8,128)S(1)} %fusion.44), channel_id=1, source_target_pairs={{0,4},{4,8},{8,12},{12,0},{1,5},{5,9},{9,13},{13,1},{2,6},{6,10},{... | collective-permute-start | bytes 786440 | tf_op jit(solution)/shard_map/while/body/eval_jaxpr/ppermute | solution.py:31
Sparse Core Ops, SparseCore 0:
  237.1 71.4 reduce-scatter.1
where the time goes:
time: 320 us; the launch traced here: 319 us
  waiting for transfers between devices  142 us (44%)
  other arithmetic  70.3 us (22%)
  matrix products  40.3 us (13%)
  local copies, waits for them, and re-layouts  28.6 us (9%)
  starting transfers between devices  22.6 us (7%)
  between operations  14.2 us (4%)
    reduce_scatter x1, waiting for transfers between devices, shards(): lax.psum_scatter(query_total, ('sub', 'pair'), scatter_dimension=0, tiled...  70.9 us
    unnamed x3, other arithmetic  45.5 us
    ppermute x2, waiting for transfers between devices, extended(): lax.ppermute(tail, axis, [(i, (i + 1) % count) for i in range(ends)])  40.4 us
    dot_general x4, matrix products, project(): lax.dot_general(block, feat_flat, (((0,), (0,)), ((), ())), preferred_ele...  28.1 us
    all_to_all x1, waiting for transfers between devices, shards(): lax.all_to_all(corr_grad, 'blk', split_axis=2, concat_axis=0, tiled=True)  25.3 us
    dot_general x4, matrix products, project(): jnp.dot(block, query_feats, preferred_element_type=jnp.float32)  12.1 us
    convert_element_type x1, other arithmetic, shards(): corr_grad = (query_pass(grad_volume, query_kernel) + support_pass(rimmed,...  11.4 us
    add x1, other arithmetic, query_pass(): total + kernel[row_shift, col_shift] * padded[:, :, row_shift:row_shift +...  9.43 us
  transfers between devices with their start and end apart: 14, of which 5 were waited for; matrix products, arithmetic and copies ran while one was open for 18% of the time, Pallas kernels for 0%

commit v1 on v0

--- a/solution.py
+++ b/solution.py
@@ -6,6 +6,18 @@
 
 QW = 128
 QH = 64
+
+
+def exchange_directly(x, axis, split, join):
+    ways, here = (lax.axis_size(axis), lax.axis_index(axis))
+    width = x.shape[split] // ways
+    turned = jnp.roll(x, -here * width, axis=split)
+    got = [lax.slice_in_dim(turned, 0, width, axis=split)]
+    for far in range(1, ways):
+        sent = lax.slice_in_dim(turned, far * width, (far + 1) * width, axis=split)
+        got.append(lax.ppermute(sent, axis, [(d, (d + far) % ways) for d in range(ways)]))
+    line = jnp.concatenate(got[::-1], axis=join)
+    return jnp.roll(line, (here + 1) * got[0].shape[join], axis=join)
 
 
 def extended(cells, sides, width):
@@ -63,7 +75,7 @@
         query_pass(grad_volume, query_kernel)
         + support_pass(rimmed, support_kernel, planes, columns)
     ).astype(jnp.bfloat16)
-    moved = lax.all_to_all(corr_grad, "blk", split_axis=2, concat_axis=0, tiled=True)
+    moved = exchange_directly(corr_grad, "blk", 2, 0)
     cycle_size = lax.axis_size("blk")
     own_index = lax.axis_index("blk")
     tile_len = moved.shape[2]

time: 320 us -> 250 us (0.78)
  other arithmetic: 70.3 us -> 25.5 us
  local copies, waits for them, and re-layouts: 28.6 us -> 6.63 us
  waiting for transfers between devices: 142 us -> 137 us
    unnamed x3 -> x2, other arithmetic: 45.5 us -> 0.24 us
    all_to_all x1 -> x0, waiting for transfers between devices: 25.3 us -> none  [shards(): lax.all_to_all(corr_grad, 'blk', split_axis=2, concat_axis=0, tiled=True)]
    ppermute x0 -> x3, waiting for transfers between devices: none -> 22.3 us  [exchange_directly(): lax.ppermute(sent, axis, [(d, (d + far) % ways) for d in range(ways)])]
    all_to_all x2 -> x0, local copies, waits for them, and re-layouts: 8.96 us -> none  [shards(): lax.all_to_all(corr_grad, 'blk', split_axis=2, concat_axis=0, tiled=True)]
    convert_element_type x1 -> x0, local copies, waits for them, and re-layouts: 6.78 us -> none  [shards(): corr_grad = (query_pass(grad_volume, query_kernel) + support_pass(rimmed,...]
    ppermute x0 -> x3, starting transfers between devices: none -> 6.72 us  [exchange_directly(): lax.ppermute(sent, axis, [(d, (d + far) % ways) for d in range(ways)])]
    all_to_all x1 -> x0, starting transfers between devices: 6.3 us -> none  [shards(): lax.all_to_all(corr_grad, 'blk', split_axis=2, concat_axis=0, tiled=True)]
    unnamed x16 -> x17, local copies, waits for them, and re-layouts: 7.52 us -> 1.27 us
  transfers between devices with their start and end apart: 14 -> 16, of which waited for: 5 -> 6; matrix products, arithmetic and copies ran while one was open for 18% -> 23% of each run, Pallas kernels for 0% -> 0%
where the time goes in v1:
time: 250 us; the launch traced here: 249 us
  waiting for transfers between devices  137 us (55%)
  matrix products  40.3 us (16%)
  starting transfers between devices  25.7 us (10%)
  other arithmetic  25.5 us (10%)
  between operations  14.3 us (6%)
  local copies, waits for them, and re-layouts  6.63 us (3%)
    reduce_scatter x1, waiting for transfers between devices, shards(): lax.psum_scatter(query_total, ('sub', 'pair'), scatter_dimension=0, tiled...  71 us
    ppermute x2, waiting for transfers between devices, extended(): lax.ppermute(tail, axis, [(i, (i + 1) % count) for i in range(ends)])  40.4 us
    dot_general x4, matrix products, project(): lax.dot_general(block, feat_flat, (((0,), (0,)), ((), ())), preferred_ele...  28.2 us
    ppermute x3, waiting for transfers between devices, exchange_directly(): lax.ppermute(sent, axis, [(d, (d + far) % ways) for d in range(ways)])  22.3 us
    dot_general x4, matrix products, project(): jnp.dot(block, query_feats, preferred_element_type=jnp.float32)  12.1 us
    convert_element_type x1, other arithmetic, shards(): corr_grad = (query_pass(grad_volume, query_kernel) + support_pass(rimmed,...  11.2 us
    ppermute x8, starting transfers between devices, shifted(): return lax.ppermute(value, axis, pairs)  10 us
    add x1, other arithmetic, query_pass(): total + kernel[row_shift, col_shift] * padded[:, :, row_shift:row_shift +...  9.59 us
  transfers between devices with their start and end apart: 16, of which 6 were waited for; matrix products, arithmetic and copies ran while one was open for 23% of the time, Pallas kernels for 0%

profile of v1, /device:TPU:0, one launch (start us, length us, event | category | flops | bytes accessed | tf_op | source)
XLA Modules:
  0.0 249.3 jit_solution(10874276899575807985)
XLA Ops:
  7.2 5.0 %collective-permute-start.2 = (bf16[1,64,8192]{2,1,0:T(8,128)(2,1)}, bf16[1,64,8192]{2,1,0:T(8,128)(2,1)S(1)}, u32[]{:S(2)}, u32[]{:S(2)}) collective-permute-start(bf16[1,64,8192]{2,1,0:T(8,128)(2,1)} %param.7), channel_id=1, source_target_pairs={{0,2},{2,4},{4,6},{6,8},{8,10},{10,12},{12,14},{1,3},{3,5},{5,7},{... | collective-permute-start | bytes 3145736 | tf_op jit(solution)/shard_map/ppermute | solution.py:31
  12.3 1.3 collective-permute-start.3
  13.6 1.7 fusion.35
  15.3 1.7 fusion.34
  17.0 40.4 %collective-permute-done.2 = bf16[1,64,8192]{2,1,0:T(8,128)(2,1)S(1)} collective-permute-done((bf16[1,64,8192]{2,1,0:T(8,128)(2,1)}, bf16[1,64,8192]{2,1,0:T(8,128)(2,1)S(1)}, u32[]{:S(2)}, u32[]{:S(2)}) %collective-permute-start.2) | collective-permute-done | bytes 1048608 | tf_op jit(solution)/shard_map/ppermute | solution.py:31
  58.0 1.3 collective-permute-start.4
  59.3 1.3 collective-permute-start.5
  61.0 9.6 %fusion.23 = f32[1,64,64,128]{3,2,1,0:T(8,128)S(1)} fusion(f32[1,64,64,128]{3,2,1,0:T(8,128)S(1)} %bitcast.50, f32[]{:T(128)} %bitcast.8, f32[]{:T(128)} %bitcast.7, f32[]{:T(128)} %bitcast.6, f32[]{:T(128)} %bitcast.5, f32[]{:T(128)} %bitcast.4, f32[]{:T(128)} %bitcast.3, f32[]{:T(128)} %bitcast.2, f32[]{:T(128)} %bitcast.1, f32[]{:T(128)} %bitcast), kind=kLoop, calls=%fused_computation.35 | loop fusion | flops 8912896 | bytes 4194340 | tf_op jit(solution)/shard_map/add | solution.py:54
  70.6 1.5 reshape.57
  72.1 11.2 %fusion.14 = bf16[1,64,8192]{2,1,0:T(8,128)(2,1)S(1)} fusion(f32[1,64,8192]{2,1,0:T(8,128)} %reshape.57, bf16[1,64,8192]{2,1,0:T(8,128)(2,1)} %param.7, bf16[1,64,8192]{2,1,0:T(8,128)(2,1)} %copy-done.2, bf16[1,64,8192]{2,1,0:T(8,128)(2,1)S(1)} %collective-permute-done.2, bf16[3,1,8192]{2,1,0:T(2,128)(2,1)S(1)} %collective-permute-done.5, ...), kind=kLoop, calls=%fused_computation.26 | loop fusion | flops 24117248 | bytes 9535524 | tf_op jit(solution)/shard_map/convert_element_type | solution.py:77
  83.9 5.7 %collective-permute-start.6 = (bf16[1,64,2048]{2,1,0:T(8,128)(2,1)S(1)}, bf16[1,64,2048]{2,1,0:T(8,128)(2,1)S(1)}, u32[]{:S(2)}, u32[]{:S(2)}) collective-permute-start(bf16[1,64,2048]{2,1,0:T(8,128)(2,1)S(1)} %get-tuple-element.224), channel_id=1, source_target_pairs={{0,12},{4,0},{8,4},{12,8},{1,13},{5,1},{9,5},{13,9},{2,14},{6,2},{... | collective-permute-start | bytes 786440 | tf_op jit(solution)/shard_map/ppermute | solution.py:18
  89.7 1.0 collective-permute-start.8
  90.7 5.6 %collective-permute-done.6 = bf16[1,64,2048]{2,1,0:T(8,128)(2,1)S(1)} collective-permute-done((bf16[1,64,2048]{2,1,0:T(8,128)(2,1)S(1)}, bf16[1,64,2048]{2,1,0:T(8,128)(2,1)S(1)}, u32[]{:S(2)}, u32[]{:S(2)}) %collective-permute-start.6) | collective-permute-done | bytes 262176 | tf_op jit(solution)/shard_map/ppermute | solution.py:18
  96.3 16.6 %collective-permute-done.7 = bf16[1,64,2048]{2,1,0:T(8,128)(2,1)S(1)} collective-permute-done((bf16[1,64,2048]{2,1,0:T(8,128)(2,1)S(1)}, bf16[1,64,2048]{2,1,0:T(8,128)(2,1)S(1)}, u32[]{:S(2)}, u32[]{:S(2)}) %collective-permute-start.7) | collective-permute-done | bytes 262176 | tf_op jit(solution)/shard_map/ppermute | solution.py:18
  114.0 53.6 %while.20 = (s32[]{:T(128)}, f32[2048,1024]{1,0:T(8,128)}, bf16[1,64,1024]{2,1,0:T(8,128)(2,1)S(1)}, f32[1,64,1024]{2,1,0:T(8,128)S(1)}, s32[]{:T(128)}, /*index...) while((s32[]{:T(128)}, f32[2048,1024]{1,0:T(8,128)}, ...), condition=%wide.region_1.2_spmd.clone, body=%wide.region_0.1_spmd.clone.sunk | while | flops 541130752 | bytes 23986536 | solution.py:110
  114.0 1.2 collective-permute-start
  115.2 3.0 %fusion.46 = f32[1,64,1024]{2,1,0:T(8,128)S(1)} fusion(f32[1,64,1024]{2,1,0:T(8,128)S(1)} %get-tuple-element.302, bf16[2048,1024]{1,0:T(8,128)(2,1)} %get-tuple-element.316, bf16[4,1,64,2048]{3,2,1,0:T(8,128)(2,1)S(1)} %get-tuple-element.315, s32[]{:T(128)S(6)} %select_n.62), kind=kOutput, calls=%fused_computation.2.clone.1 | convolution fusion | flops 268500992 | bytes 4980740 | tf_op jit(solution)/shard_map/while/body/eval_jaxpr/dot_general | solution.py:93
  118.2 2.5 %collective-permute-start.1 = (f32[1,64,1024]{2,1,0:T(8,128)S(1)}, f32[1,64,1024]{2,1,0:T(8,128)S(1)}, u32[]{:S(2)}, u32[]{:S(2)}) collective-permute-start(f32[1,64,1024]{2,1,0:T(8,128)S(1)} %fusion.46), channel_id=1, source_target_pairs={{0,4},{4,8},{8,12},{12,0},{1,5},{5,9},{9,13},{13,1},{2,6},{6,10},{... | collective-permute-start | bytes 786440 | tf_op jit(solution)/shard_map/while/body/eval_jaxpr/ppermute | solution.py:43
  120.8 4.5 %select_add_fusion.2 = f32[2048,1024]{1,0:T(8,128)} fusion(f32[2048,1024]{1,0:T(8,128)} %get-tuple-element.300, pred[]{:T(512)S(6)} %compare.7, bf16[4,1,64,2048]{3,2,1,0:T(8,128)(2,1)S(1)} %get-tuple-element.315, s32[]{:T(128)S(6)} %select_n.62, bf16[1,64,1024]{2,1,0:T(8,128)(2,1)S(1)} %copy.23), kind=kOutput, calls=%fused_computation.clone.1 | convolution fusion | flops 272629760 | bytes 17170436 | tf_op jit(solution)/shard_map/while/body/eval_jaxpr/dot_general | solution.py:90
  125.3 2.7 %collective-permute-done.1 = f32[1,64,1024]{2,1,0:T(8,128)S(1)} collective-permute-done((f32[1,64,1024]{2,1,0:T(8,128)S(1)}, f32[1,64,1024]{2,1,0:T(8,128)S(1)}, u32[]{:S(2)}, u32[]{:S(2)}) %collective-permute-start.1) | collective-permute-done | bytes 262176 | tf_op jit(solution)/shard_map/while/body/eval_jaxpr/ppermute | solution.py:43
  128.7 3.0 %fusion.46 = f32[1,64,1024]{2,1,0:T(8,128)S(1)} fusion(f32[1,64,1024]{2,1,0:T(8,128)S(1)} %get-tuple-element.302, bf16[2048,1024]{1,0:T(8,128)(2,1)} %get-tuple-element.316, bf16[4,1,64,2048]{3,2,1,0:T(8,128)(2,1)S(1)} %get-tuple-element.315, s32[]{:T(128)S(6)} %select_n.62), kind=kOutput, calls=%fused_computation.2.clone.1 | convolution fusion | flops 268500992 | bytes 4980740 | tf_op jit(solution)/shard_map/while/body/eval_jaxpr/dot_general | solution.py:93
  132.2 7.9 %select_add_fusion.2 = f32[2048,1024]{1,0:T(8,128)} fusion(f32[2048,1024]{1,0:T(8,128)} %get-tuple-element.300, pred[]{:T(512)S(6)} %compare.7, bf16[4,1,64,2048]{3,2,1,0:T(8,128)(2,1)S(1)} %get-tuple-element.315, s32[]{:T(128)S(6)} %select_n.62, bf16[1,64,1024]{2,1,0:T(8,128)(2,1)S(1)} %copy.23), kind=kOutput, calls=%fused_computation.clone.1 | convolution fusion | flops 272629760 | bytes 17170436 | tf_op jit(solution)/shard_map/while/body/eval_jaxpr/dot_general | solution.py:90
  140.5 0.8 collective-permute-start
  141.2 3.0 %fusion.46 = f32[1,64,1024]{2,1,0:T(8,128)S(1)} fusion(f32[1,64,1024]{2,1,0:T(8,128)S(1)} %get-tuple-element.302, bf16[2048,1024]{1,0:T(8,128)(2,1)} %get-tuple-element.316, bf16[4,1,64,2048]{3,2,1,0:T(8,128)(2,1)S(1)} %get-tuple-element.315, s32[]{:T(128)S(6)} %select_n.62), kind=kOutput, calls=%fused_computation.2.clone.1 | convolution fusion | flops 268500992 | bytes 4980740 | tf_op jit(solution)/shard_map/while/body/eval_jaxpr/dot_general | solution.py:93
  144.3 2.9 %collective-permute-start.1 = (f32[1,64,1024]{2,1,0:T(8,128)S(1)}, f32[1,64,1024]{2,1,0:T(8,128)S(1)}, u32[]{:S(2)}, u32[]{:S(2)}) collective-permute-start(f32[1,64,1024]{2,1,0:T(8,128)S(1)} %fusion.46), channel_id=1, source_target_pairs={{0,4},{4,8},{8,12},{12,0},{1,5},{5,9},{9,13},{13,1},{2,6},{6,10},{... | collective-permute-start | bytes 786440 | tf_op jit(solution)/shard_map/while/body/eval_jaxpr/ppermute | solution.py:43
  147.2 7.9 %select_add_fusion.2 = f32[2048,1024]{1,0:T(8,128)} fusion(f32[2048,1024]{1,0:T(8,128)} %get-tuple-element.300, pred[]{:T(512)S(6)} %compare.7, bf16[4,1,64,2048]{3,2,1,0:T(8,128)(2,1)S(1)} %get-tuple-element.315, s32[]{:T(128)S(6)} %select_n.62, bf16[1,64,1024]{2,1,0:T(8,128)(2,1)S(1)} %copy.23), kind=kOutput, calls=%fused_computation.clone.1 | convolution fusion | flops 272629760 | bytes 17170436 | tf_op jit(solution)/shard_map/while/body/eval_jaxpr/dot_general | solution.py:90
  155.1 0.7 collective-permute-start
  155.8 3.0 %fusion.46 = f32[1,64,1024]{2,1,0:T(8,128)S(1)} fusion(f32[1,64,1024]{2,1,0:T(8,128)S(1)} %get-tuple-element.302, bf16[2048,1024]{1,0:T(8,128)(2,1)} %get-tuple-element.316, bf16[4,1,64,2048]{3,2,1,0:T(8,128)(2,1)S(1)} %get-tuple-element.315, s32[]{:T(128)S(6)} %select_n.62), kind=kOutput, calls=%fused_computation.2.clone.1 | convolution fusion | flops 268500992 | bytes 4980740 | tf_op jit(solution)/shard_map/while/body/eval_jaxpr/dot_general | solution.py:93
  158.9 0.8 collective-permute-start.1
  159.6 7.9 %select_add_fusion.2 = f32[2048,1024]{1,0:T(8,128)} fusion(f32[2048,1024]{1,0:T(8,128)} %get-tuple-element.300, pred[]{:T(512)S(6)} %compare.7, bf16[4,1,64,2048]{3,2,1,0:T(8,128)(2,1)S(1)} %get-tuple-element.315, s32[]{:T(128)S(6)} %select_n.62, bf16[1,64,1024]{2,1,0:T(8,128)(2,1)S(1)} %copy.23), kind=kOutput, calls=%fused_computation.clone.1 | convolution fusion | flops 272629760 | bytes 17170436 | tf_op jit(solution)/shard_map/while/body/eval_jaxpr/dot_general | solution.py:90
  168.3 71.0 %reduce-scatter.2.cloned.1.call-done = f32[512,1024]{1,0:T(8,128)} async-done(((f32[2048,1024]{1,0:T(8,128)}), f32[512,1024]{1,0:T(8,128)}) %reduce-scatter.2.cloned.1.call-update) | async-done | bytes 2097168 | tf_op jit(solution)/shard_map/reduce_scatter | solution.py:112
  239.3 3.2 %broadcast_multiply_fusion = f32[512,1024]{1,0:T(8,128)} fusion(f32[512,1024]{1,0:T(8,128)} %reduce-scatter.2.cloned.1.call-done), kind=kLoop, calls=%fused_computation.48 | loop fusion | flops 524288 | bytes 4194304 | tf_op jit(solution)/shard_map/mul | solution.py:112
  (47 shorter events, 4.9 us)
Async XLA Ops:
  7.2 50.3 %copy-start.3 = (bf16[1,64,8192]{2,1,0:T(8,128)(2,1)S(1)}, bf16[1,64,8192]{2,1,0:T(8,128)(2,1)}, u32[]{:S(2)}) copy-start(bf16[1,64,8192]{2,1,0:T(8,128)(2,1)} %param.7) | copy-start | bytes 3145732
  7.2 232.1 %reduce-scatter.2.cloned.1.call-start = ((), (), s32[]{:S(2)}) async-start(), calls=%async_computation.1 | async-start | bytes 10485760 | tf_op jit(solution)/shard_map/reduce_scatter | solution.py:112
  7.2 50.2 %collective-permute-start.2 = (bf16[1,64,8192]{2,1,0:T(8,128)(2,1)}, bf16[1,64,8192]{2,1,0:T(8,128)(2,1)S(1)}, u32[]{:S(2)}, u32[]{:S(2)}) collective-permute-start(bf16[1,64,8192]{2,1,0:T(8,128)(2,1)} %param.7), channel_id=1, source_target_pairs={{0,2},{2,4},{4,6},{6,8},{8,10},{10,12},{12,14},{1,3},{3,5},{5,7},{... | collective-permute-start | bytes 3145736 | tf_op jit(solution)/shard_map/ppermute | solution.py:31
  12.3 45.5 %collective-permute-start.3 = (bf16[1,64,8192]{2,1,0:T(8,128)(2,1)}, bf16[1,64,8192]{2,1,0:T(8,128)(2,1)S(1)}, u32[]{:S(2)}, u32[]{:S(2)}) collective-permute-start(bf16[1,64,8192]{2,1,0:T(8,128)(2,1)} %param.7), channel_id=1, source_target_pairs={{2,0},{4,2},{6,4},{8,6},{10,8},{12,10},{14,12},{3,1},{5,3},{7,5},{... | collective-permute-start | bytes 3145736 | tf_op jit(solution)/shard_map/ppermute | solution.py:33
  57.7 3.2 %copy-start.2 = (bf16[1,64,8192]{2,1,0:T(8,128)(2,1)}, bf16[1,64,8192]{2,1,0:T(8,128)(2,1)S(1)}, u32[]{:S(2)}) copy-start(bf16[1,64,8192]{2,1,0:T(8,128)(2,1)S(1)} %collective-permute-done.3) | copy-start | bytes 3145732
  57.8 3.2 %copy-start = (bf16[3,64,8192]{2,1,0:T(8,128)(2,1)}, bf16[3,64,8192]{2,1,0:T(8,128)(2,1)S(1)}, u32[]{:S(2)}) copy-start(bf16[3,64,8192]{2,1,0:T(8,128)(2,1)S(1)} %constant_dynamic-update-slice_fusion) | copy-start | bytes 9437188
  58.0 14.1 %collective-permute-start.4 = (bf16[3,1,8192]{2,1,0:T(2,128)(2,1)S(1)}, bf16[3,1,8192]{2,1,0:T(2,128)(2,1)S(1)}, u32[]{:S(2)}, u32[]{:S(2)}) collective-permute-start(bf16[3,1,8192]{2,1,0:T(2,128)(2,1)S(1)} %get-tuple-element.220), channel_id=1, source_target_pairs={{0,1},{2,3},{4,5},{6,7},{8,9},{10,11},{12,13},{14,15},{16,17},{18,... | collective-permute-start | bytes 147464 | tf_op jit(solution)/shard_map/ppermute | solution.py:31
  59.3 12.8 %collective-permute-start.5 = (bf16[3,1,8192]{2,1,0:T(2,128)(2,1)S(1)}, bf16[3,1,8192]{2,1,0:T(2,128)(2,1)S(1)}, u32[]{:S(2)}, u32[]{:S(2)}) collective-permute-start(bf16[3,1,8192]{2,1,0:T(2,128)(2,1)S(1)} %get-tuple-element.221), channel_id=1, source_target_pairs={{1,0},{3,2},{5,4},{7,6},{9,8},{11,10},{13,12},{15,14},{17,16},{19,... | collective-permute-start | bytes 147464 | tf_op jit(solution)/shard_map/ppermute | solution.py:33
  83.9 12.3 %collective-permute-start.6 = (bf16[1,64,2048]{2,1,0:T(8,128)(2,1)S(1)}, bf16[1,64,2048]{2,1,0:T(8,128)(2,1)S(1)}, u32[]{:S(2)}, u32[]{:S(2)}) collective-permute-start(bf16[1,64,2048]{2,1,0:T(8,128)(2,1)S(1)} %get-tuple-element.224), channel_id=1, source_target_pairs={{0,12},{4,0},{8,4},{12,8},{1,13},{5,1},{9,5},{13,9},{2,14},{6,2},{... | collective-permute-start | bytes 786440 | tf_op jit(solution)/shard_map/ppermute | solution.py:18
  89.7 23.3 %collective-permute-start.7 = (bf16[1,64,2048]{2,1,0:T(8,128)(2,1)S(1)}, bf16[1,64,2048]{2,1,0:T(8,128)(2,1)S(1)}, u32[]{:S(2)}, u32[]{:S(2)}) collective-permute-start(bf16[1,64,2048]{2,1,0:T(8,128)(2,1)S(1)} %get-tuple-element.223), channel_id=1, source_target_pairs={{0,8},{4,12},{8,0},{12,4},{1,9},{5,13},{9,1},{13,5},{2,10},{6,14},... | collective-permute-start | bytes 786440 | tf_op jit(solution)/shard_map/ppermute | solution.py:18
  89.7 23.3 %collective-permute-start.8 = (bf16[1,64,2048]{2,1,0:T(8,128)(2,1)S(1)}, bf16[1,64,2048]{2,1,0:T(8,128)(2,1)S(1)}, u32[]{:S(2)}, u32[]{:S(2)}) collective-permute-start(bf16[1,64,2048]{2,1,0:T(8,128)(2,1)S(1)} %get-tuple-element.222), channel_id=1, source_target_pairs={{0,4},{4,8},{8,12},{12,0},{1,5},{5,9},{9,13},{13,1},{2,6},{6,10},{... | collective-permute-start | bytes 786440 | tf_op jit(solution)/shard_map/ppermute | solution.py:18
  113.1 0.9 copy-start.1
  114.0 11.3 %collective-permute-start = (bf16[1,64,1024]{2,1,0:T(8,128)(2,1)S(1)}, bf16[1,64,1024]{2,1,0:T(8,128)(2,1)S(1)}, u32[]{:S(2)}, u32[]{:S(2)}) collective-permute-start(bf16[1,64,1024]{2,1,0:T(8,128)(2,1)S(1)} %copy.23), channel_id=1, source_target_pairs={{0,4},{4,8},{8,12},{12,0},{1,5},{5,9},{9,13},{13,1},{2,6},{6,10},{... | collective-permute-start | bytes 393224 | tf_op jit(solution)/shard_map/while/body/eval_jaxpr/ppermute | solution.py:43
  118.2 9.8 %collective-permute-start.1 = (f32[1,64,1024]{2,1,0:T(8,128)S(1)}, f32[1,64,1024]{2,1,0:T(8,128)S(1)}, u32[]{:S(2)}, u32[]{:S(2)}) collective-permute-start(f32[1,64,1024]{2,1,0:T(8,128)S(1)} %fusion.46), channel_id=1, source_target_pairs={{0,4},{4,8},{8,12},{12,0},{1,5},{5,9},{9,13},{13,1},{2,6},{6,10},{... | collective-permute-start | bytes 786440 | tf_op jit(solution)/shard_map/while/body/eval_jaxpr/ppermute | solution.py:43
  128.0 12.0 %collective-permute-start = (bf16[1,64,1024]{2,1,0:T(8,128)(2,1)S(1)}, bf16[1,64,1024]{2,1,0:T(8,128)(2,1)S(1)}, u32[]{:S(2)}, u32[]{:S(2)}) collective-permute-start(bf16[1,64,1024]{2,1,0:T(8,128)(2,1)S(1)} %copy.23), channel_id=1, source_target_pairs={{0,4},{4,8},{8,12},{12,0},{1,5},{5,9},{9,13},{13,1},{2,6},{6,10},{... | collective-permute-start | bytes 393224 | tf_op jit(solution)/shard_map/while/body/eval_jaxpr/ppermute | solution.py:43
  131.8 8.7 %collective-permute-start.1 = (f32[1,64,1024]{2,1,0:T(8,128)S(1)}, f32[1,64,1024]{2,1,0:T(8,128)S(1)}, u32[]{:S(2)}, u32[]{:S(2)}) collective-permute-start(f32[1,64,1024]{2,1,0:T(8,128)S(1)} %fusion.46), channel_id=1, source_target_pairs={{0,4},{4,8},{8,12},{12,0},{1,5},{5,9},{9,13},{13,1},{2,6},{6,10},{... | collective-permute-start | bytes 786440 | tf_op jit(solution)/shard_map/while/body/eval_jaxpr/ppermute | solution.py:43
  140.5 14.6 %collective-permute-start = (bf16[1,64,1024]{2,1,0:T(8,128)(2,1)S(1)}, bf16[1,64,1024]{2,1,0:T(8,128)(2,1)S(1)}, u32[]{:S(2)}, u32[]{:S(2)}) collective-permute-start(bf16[1,64,1024]{2,1,0:T(8,128)(2,1)S(1)} %copy.23), channel_id=1, source_target_pairs={{0,4},{4,8},{8,12},{12,0},{1,5},{5,9},{9,13},{13,1},{2,6},{6,10},{... | collective-permute-start | bytes 393224 | tf_op jit(solution)/shard_map/while/body/eval_jaxpr/ppermute | solution.py:43
  144.3 10.8 %collective-permute-start.1 = (f32[1,64,1024]{2,1,0:T(8,128)S(1)}, f32[1,64,1024]{2,1,0:T(8,128)S(1)}, u32[]{:S(2)}, u32[]{:S(2)}) collective-permute-start(f32[1,64,1024]{2,1,0:T(8,128)S(1)} %fusion.46), channel_id=1, source_target_pairs={{0,4},{4,8},{8,12},{12,0},{1,5},{5,9},{9,13},{13,1},{2,6},{6,10},{... | collective-permute-start | bytes 786440 | tf_op jit(solution)/shard_map/while/body/eval_jaxpr/ppermute | solution.py:43
  155.1 12.4 %collective-permute-start = (bf16[1,64,1024]{2,1,0:T(8,128)(2,1)S(1)}, bf16[1,64,1024]{2,1,0:T(8,128)(2,1)S(1)}, u32[]{:S(2)}, u32[]{:S(2)}) collective-permute-start(bf16[1,64,1024]{2,1,0:T(8,128)(2,1)S(1)} %copy.23), channel_id=1, source_target_pairs={{0,4},{4,8},{8,12},{12,0},{1,5},{5,9},{9,13},{13,1},{2,6},{6,10},{... | collective-permute-start | bytes 393224 | tf_op jit(solution)/shard_map/while/body/eval_jaxpr/ppermute | solution.py:43
  158.9 8.7 %collective-permute-start.1 = (f32[1,64,1024]{2,1,0:T(8,128)S(1)}, f32[1,64,1024]{2,1,0:T(8,128)S(1)}, u32[]{:S(2)}, u32[]{:S(2)}) collective-permute-start(f32[1,64,1024]{2,1,0:T(8,128)S(1)} %fusion.46), channel_id=1, source_target_pairs={{0,4},{4,8},{8,12},{12,0},{1,5},{5,9},{9,13},{13,1},{2,6},{6,10},{... | collective-permute-start | bytes 786440 | tf_op jit(solution)/shard_map/while/body/eval_jaxpr/ppermute | solution.py:43
Sparse Core Ops, SparseCore 0:
  167.7 71.5 reduce-scatter.1
